TPU v7x, 32 devices: a whole 2x2x4 slice. The times are simulated.
32 devices in a mesh: ens: 2 (over y), row: 4 (over z), col: 4 (over x, core).
Axes of the slice: x: 2, y: 2, z: 4, core: 2. Of those that a mesh axis runs over, the one named last changes fastest.
Arguments:
- series: float32 [24576, 256], P(('ens', 'row', 'col')), parts along dimension 0, may hold values from -22 to 22, as said below
- vectors: float32 [24576, 128], P(('ens', 'row', 'col')), parts along dimension 0, may hold values from -6 to 6
- damp_class: int32 [24576], P(('ens', 'row', 'col')), parts along dimension 0, may hold values from 0 to 15
- damp_levels: float32 [16], replicated, may hold values from 0.5 to 2
- removed_blocks: int32 [64, 32], P('ens'), parts along dimension 0, may hold values 0 or 1
Outputs:
- filtered: float32 [24576, 128], P(('ens', 'row', 'col')), parts along dimension 0
There are 2 independent parts, one for each index of `ens`. A program takes and returns all parts, laid end to end along the dimension named above; an argument that names none is the same for every part. Nothing has to cross between parts.
Inputs may be any that keep to these rules, and one draw needn't show every extreme that they name: Each voxel's series is not constant.
All inputs are finite; a program needn't handle non-finite values.
Results may differ from a plain program's by a relative error of at most 0.0003.
Values sent between devices are 32-bit elements; how exact they have to be, the bound alone decides.
No kernel may reach another device: no remote copies, remote signals or barrier semaphores. Data moves between devices by JAX's collectives and lax.ppermute only.
A program may use at most 128 MiB of HBM per device.

v0:
```python
import jax
import jax.numpy as jnp
from jax import lax
from jax.sharding import PartitionSpec as P

N = 12288
sharpness = 12.0


def standardize(series):
    centered = series - jnp.mean(series, axis=1, keepdims=True)
    spread = jnp.mean(centered * centered, axis=1, keepdims=True)
    return centered * lax.rsqrt(spread + 1e-05)


def local(series, vectors, damp_class, damp_levels, removed_blocks):
    n_col = lax.axis_size("col")
    row_id = lax.axis_index("row")
    col_id = lax.axis_index("col")
    shard_rows = series.shape[0]
    samples = series.shape[1]
    classes = damp_levels.shape[0]
    z_own = standardize(series)
    onehot = (damp_class[:, None] == jnp.arange(classes, dtype=jnp.int32)[None, :]).astype(
        jnp.float32
    )
    damping = jnp.sum(onehot * damp_levels[None, :], axis=1)
    z_rows, d_rows = (
        lax.all_gather(z_own, "col", axis=0, tiled=True),
        lax.all_gather(damping, "col", axis=0, tiled=True),
    )
    tile_rows = z_rows.shape[0]
    blocks = removed_blocks.shape[0]
    block_size = N // blocks
    row_blocks = tile_rows // block_size
    keep_rows = 1.0 - lax.dynamic_slice_in_dim(
        removed_blocks, row_id * row_blocks, row_blocks, 0
    ).astype(jnp.float32)
    shard_piece = lax.all_gather(z_own, "row", axis=0, tiled=True)
    count = shard_piece.shape[0]
    position = jnp.arange(count, dtype=jnp.int32)
    owner_row = position // shard_rows
    global_index = (owner_row * n_col + col_id) * shard_rows + position % shard_rows
    col_block = global_index // block_size
    onehot_cols = (col_block[None, :] == jnp.arange(blocks, dtype=jnp.int32)[:, None]).astype(
        jnp.float32
    )
    keep_small = jnp.dot(
        keep_rows, onehot_cols, precision=lax.Precision.HIGHEST, preferred_element_type=jnp.float32
    )
    keep_full = jnp.broadcast_to(keep_small[:, None, :], (row_blocks, block_size, count)).reshape(
        tile_rows, count
    )
    correlation = (
        lax.dot_general(
            z_rows,
            shard_piece,
            (((1,), (1,)), ((), ())),
            precision=lax.Precision.HIGHEST,
            preferred_element_type=jnp.float32,
        )
        / samples
    )
    affinity = jnp.tanh(sharpness * correlation) * keep_full * d_rows[:, None]
    spectral_scale = 0.5 * N * jnp.mean(damp_levels * damp_levels)

    def forward_add(shard_piece):
        return jnp.dot(
            affinity,
            shard_piece,
            precision=lax.Precision.HIGHEST,
            preferred_element_type=jnp.float32,
        )

    def backward_add(shard_piece):
        return lax.dot_general(
            affinity,
            shard_piece,
            (((0,), (0,)), ((), ())),
            precision=lax.Precision.HIGHEST,
            preferred_element_type=jnp.float32,
        )

    def normal_apply(field_in):
        product = forward_add(lax.all_gather(field_in, "row", axis=0, tiled=True))
        product = lax.psum_scatter(product, "col", scatter_dimension=0, tiled=True)
        returned = backward_add(lax.all_gather(product, "col", axis=0, tiled=True))
        return lax.psum_scatter(returned, "row", scatter_dimension=0, tiled=True) / spectral_scale

    first_term = normal_apply(vectors) - vectors
    filtered = 2.0 * (normal_apply(first_term) - first_term) - vectors
    return filtered


def solution(mesh):
    placed = (
        P(("ens", "row", "col"), None),
        P(("ens", "row", "col"), None),
        P(("ens", "row", "col")),
        P(),
        P("ens", None),
    )
    return jax.shard_map(
        local, mesh=mesh, in_specs=placed, out_specs=P(("ens", "row", "col"), None), check_vma=False
    )
```

profile of v0, /device:TPU:0, one launch (start us, length us, event | category | flops | bytes accessed | tf_op | source)
XLA Modules:
  0.0 560.3 jit_solution(4432875654553335063)
XLA Ops:
  6.5 1.3 reduce_sum.36
  7.9 1.4 multiply_reduce_fusion
  9.3 2.3 subtract_multiply_fusion
  11.6 0.0 all-gather.8.cloned.1.call-start
  11.7 0.7 all-gather.8.cloned.1.call-update
  12.4 0.7 all-gather.12.cloned.1.call-update
  13.1 0.0 reduce-scatter.5.cloned.1.call-start
  13.2 0.1 select_reduce_fusion
  13.3 6.2 %all-gather = f32[4,1,768]{2,1,0:T(1,128)S(1)} all-gather(f32[1,1,768]{2,1,0:T(1,128)S(1)} %reshape.49), channel_id=1, replica_groups=mesh['ens'=2,'row'=4,'col'=4] {'col'}, dimensions={0}, use_global_device_ids=true | all-gather | bytes 15360 | tf_op jit(solution)/shard_map/all_gather | solution.py:30
  19.5 0.9 fusion.1
  20.5 57.5 %all-gather.10.cloned.1.call-done = f32[3072,256]{1,0:T(8,128)} async-done(((f32[768,256]{1,0:T(8,128)}), f32[3072,256]{1,0:T(8,128)}) %all-gather.10.cloned.1.call-update) | async-done | bytes 3145744 | tf_op jit(solution)/shard_map/all_gather | solution.py:39
  78.0 28.7 %all-gather.8.cloned.1.call-done = f32[3072,256]{1,0:T(8,128)} async-done(((f32[768,256]{1,0:T(8,128)}), f32[3072,256]{1,0:T(8,128)}) %all-gather.8.cloned.1.call-update) | async-done | bytes 3145744 | tf_op jit(solution)/shard_map/all_gather | solution.py:29
  106.7 40.0 %fusion = f32[3072,3072]{1,0:T(8,128)} fusion(f32[3072,256]{1,0:T(8,128)} %all-gather.8.cloned.1.call-done, f32[3072,256]{1,0:T(8,128)} %all-gather.10.cloned.1.call-done, f32[3072]{0:T(1024)S(1)} %bitcast.15, f32[8,3072]{1,0:T(8,128)S(1)} %fusion.1), kind=kOutput, calls=%fused_computation.1 | convolution fusion | flops 29019340800 | bytes 44150784 | tf_op jit(solution)/shard_map/dot_general | solution.py:55
  146.7 34.9 %fusion.21 = f32[3072,128]{1,0:T(8,128)} fusion(f32[3072,3072]{1,0:T(8,128)} %fusion, f32[3072,128]{1,0:T(8,128)} %all-gather.12.cloned.1.call-done), kind=kOutput, calls=%fused_computation.39 | convolution fusion | flops 14495514624 | bytes 40894464 | tf_op jit(solution)/shard_map/dot_general | solution.py:68
  181.6 0.0 all-gather.14.cloned.1.call-start
  181.7 28.1 %reduce-scatter.5.cloned.1.call-done = f32[768,128]{1,0:T(8,128)} async-done(((f32[3072,128]{1,0:T(8,128)}), f32[768,128]{1,0:T(8,128)}) %reduce-scatter.5.cloned.1.call-update) | async-done | bytes 393232 | tf_op jit(solution)/shard_map/reduce_scatter | solution.py:86
  209.8 0.0 reduce-scatter.7.cloned.1.call-start
  209.9 21.0 %all-gather.14.cloned.1.call-done = f32[3072,128]{1,0:T(8,128)} async-done(((f32[768,128]{1,0:T(8,128)}), f32[3072,128]{1,0:T(8,128)}) %all-gather.14.cloned.1.call-update) | async-done | bytes 1572880 | tf_op jit(solution)/shard_map/all_gather | solution.py:87
  230.9 64.5 %fusion.22 = f32[3072,128]{1,0:T(8,128)} fusion(f32[3072,3072]{1,0:T(8,128)} %fusion, f32[3072,128]{1,0:T(8,128)} %all-gather.14.cloned.1.call-done), kind=kOutput, calls=%fused_computation.40 | convolution fusion | flops 14495514624 | bytes 40894464 | tf_op jit(solution)/shard_map/dot_general | solution.py:76
  295.4 0.0 all-gather.16.cloned.1.call-start
  295.5 0.6 multiply_reduce_fusion.1
  296.7 34.3 %reduce-scatter.7.cloned.1.call-done = f32[768,128]{1,0:T(8,128)} async-done(((f32[3072,128]{1,0:T(8,128)}), f32[768,128]{1,0:T(8,128)}) %reduce-scatter.7.cloned.1.call-update) | async-done | bytes 393232 | tf_op jit(solution)/shard_map/reduce_scatter | solution.py:88
  331.0 1.8 divide_subtract_fusion
  332.8 0.0 reduce-scatter.9.cloned.1.call-start
  332.9 36.0 %all-gather.16.cloned.1.call-done = f32[3072,128]{1,0:T(8,128)} async-done(((f32[768,128]{1,0:T(8,128)}), f32[3072,128]{1,0:T(8,128)}) %all-gather.16.cloned.1.call-update) | async-done | bytes 1572880 | tf_op jit(solution)/shard_map/all_gather | solution.py:85
  368.8 34.7 %fusion.23 = f32[3072,128]{1,0:T(8,128)} fusion(f32[3072,3072]{1,0:T(8,128)} %fusion, f32[3072,128]{1,0:T(8,128)} %all-gather.16.cloned.1.call-done), kind=kOutput, calls=%fused_computation.41 | convolution fusion | flops 14495514624 | bytes 40894464 | tf_op jit(solution)/shard_map/dot_general | solution.py:68
  403.6 0.0 all-gather.18.cloned.1.call-start
  403.6 27.0 %reduce-scatter.9.cloned.1.call-done = f32[768,128]{1,0:T(8,128)} async-done(((f32[3072,128]{1,0:T(8,128)}), f32[768,128]{1,0:T(8,128)}) %reduce-scatter.9.cloned.1.call-update) | async-done | bytes 393232 | tf_op jit(solution)/shard_map/reduce_scatter | solution.py:86
  430.7 21.1 %all-gather.18.cloned.1.call-done = f32[3072,128]{1,0:T(8,128)} async-done(((f32[768,128]{1,0:T(8,128)}), f32[3072,128]{1,0:T(8,128)}) %all-gather.18.cloned.1.call-update) | async-done | bytes 1572880 | tf_op jit(solution)/shard_map/all_gather | solution.py:87
  451.8 64.0 %fusion.24 = f32[3072,128]{1,0:T(8,128)} fusion(f32[3072,3072]{1,0:T(8,128)} %fusion, f32[3072,128]{1,0:T(8,128)} %all-gather.18.cloned.1.call-done), kind=kOutput, calls=%fused_computation.42 | convolution fusion | flops 14495514624 | bytes 40894464 | tf_op jit(solution)/shard_map/dot_general | solution.py:76
  515.9 35.6 %reduce-scatter.11.cloned.1.call-done = f32[768,128]{1,0:T(8,128)} async-done(((f32[3072,128]{1,0:T(8,128)}), f32[768,128]{1,0:T(8,128)}) %reduce-scatter.11.cloned.1.call-update) | async-done | bytes 393232 | tf_op jit(solution)/shard_map/reduce_scatter | solution.py:88
  551.5 1.8 multiply_subtract_fusion
  (24 shorter events, 0.3 us)
Async XLA Ops:
  6.5 6.6 %copy-start.2 = (s32[768]{0:T(1024)S(1)}, s32[768]{0:T(1024)}, u32[]{:S(2)}) copy-start(s32[768]{0:T(1024)} %param.7) | copy-start | bytes 9220
  6.5 6.7 %copy-start.3 = (f32[16]{0:T(128)S(1)}, f32[16]{0:T(128)}, u32[]{:S(2)}) copy-start(f32[16]{0:T(128)} %param.8) | copy-start | bytes 196
  6.5 71.4 %all-gather.10.cloned.1.call-start = ((), (), s32[]{:S(2)}) async-start(), calls=%async_computation.5 | async-start | bytes 3932160 | tf_op jit(solution)/shard_map/all_gather | solution.py:39
  11.6 95.1 %all-gather.8.cloned.1.call-start = ((), (), s32[]{:S(2)}) async-start(), calls=%async_computation.4 | async-start | bytes 3932160 | tf_op jit(solution)/shard_map/all_gather | solution.py:29
  12.4 134.3 %all-gather.12.cloned.1.call-start = ((), (), s32[]{:S(2)}) async-start(), calls=%async_computation.6 | async-start | bytes 1966080 | tf_op jit(solution)/shard_map/all_gather | solution.py:85
  13.1 196.7 %reduce-scatter.5.cloned.1.call-start = ((), (), s32[]{:S(2)}) async-start(), calls=%async_computation.7 | async-start | bytes 1966080 | tf_op jit(solution)/shard_map/reduce_scatter | solution.py:86
  181.6 49.3 %all-gather.14.cloned.1.call-start = ((), (), s32[]{:S(2)}) async-start(), calls=%async_computation.8 | async-start | bytes 1966080 | tf_op jit(solution)/shard_map/all_gather | solution.py:87
  209.8 121.2 %copy-start = (f32[768,128]{1,0:T(8,128)S(1)}, f32[768,128]{1,0:T(8,128)}, u32[]{:S(2)}) copy-start(f32[768,128]{1,0:T(8,128)} %param.6) | copy-start | bytes 1179652
  209.8 121.2 %reduce-scatter.7.cloned.1.call-start = ((), (), s32[]{:S(2)}) async-start(), calls=%async_computation.9 | async-start | bytes 1966080 | tf_op jit(solution)/shard_map/reduce_scatter | solution.py:88
  295.4 73.4 %all-gather.16.cloned.1.call-start = ((), (), s32[]{:S(2)}) async-start(), calls=%async_computation.10 | async-start | bytes 1966080 | tf_op jit(solution)/shard_map/all_gather | solution.py:85
  332.8 97.8 %reduce-scatter.9.cloned.1.call-start = ((), (), s32[]{:S(2)}) async-start(), calls=%async_computation.11 | async-start | bytes 1966080 | tf_op jit(solution)/shard_map/reduce_scatter | solution.py:86
  403.6 48.2 %all-gather.18.cloned.1.call-start = ((), (), s32[]{:S(2)}) async-start(), calls=%async_computation.12 | async-start | bytes 1966080 | tf_op jit(solution)/shard_map/all_gather | solution.py:87
  430.6 120.8 %copy-start.1 = (f32[768,128]{1,0:T(8,128)S(1)}, f32[768,128]{1,0:T(8,128)}, u32[]{:S(2)}) copy-start(f32[768,128]{1,0:T(8,128)} %reduce-scatter.7.cloned.1.call-done) | copy-start | bytes 1179652
  430.6 120.8 %reduce-scatter.11.cloned.1.call-start = ((), (), s32[]{:S(2)}) async-start(), calls=%async_computation.13 | async-start | bytes 1966080 | tf_op jit(solution)/shard_map/reduce_scatter | solution.py:88
Sparse Core Ops, SparseCore 0:
  11.8 66.1 all-gather.9
  79.5 27.1 all-gather.7
  108.3 37.0 all-gather.11
  181.7 28.0 reduce-scatter.4
  211.2 19.6 all-gather.13
  295.5 35.4 reduce-scatter.6
  332.9 35.8 all-gather.15
  403.7 26.8 reduce-scatter.8
  432.2 19.6 all-gather.17
  516.0 35.4 reduce-scatter.10
where the time goes:
time: 568 us; the launch traced here: 560 us
  waiting for transfers between devices  291 us (51%)
  matrix products  239 us (42%)
  between operations  14.5 us (3%)
  other arithmetic  9.36 us (2%)
  blocking collectives  6.21 us (1%)
    dot_general x2, matrix products, backward_add(): lax.dot_general(affinity, shard_piece, (((0,), (0,)), ((), ())), precisio...  129 us
    reduce_scatter x2, waiting for transfers between devices, normal_apply(): lax.psum_scatter(returned, 'row', scatter_dimension=0, tiled=True)  69.9 us
    dot_general x2, matrix products, forward_add(): jnp.dot(affinity, shard_piece, precision=lax.Precision.HIGHEST, preferred...  69.6 us
    all_gather x1, waiting for transfers between devices, local(): shard_piece = lax.all_gather(z_own, 'row', axis=0, tiled=True)  57.5 us
    reduce_scatter x2, waiting for transfers between devices, normal_apply(): product = lax.psum_scatter(product, 'col', scatter_dimension=0, tiled=True)  55.1 us
    all_gather x2, waiting for transfers between devices, normal_apply(): returned = backward_add(lax.all_gather(product, 'col', axis=0, tiled=True))  42.1 us
    dot_general x1, matrix products, local(): lax.dot_general(z_rows, shard_piece, (((1,), (1,)), ((), ())), precision=...  40 us
    all_gather x2, waiting for transfers between devices, normal_apply(): product = forward_add(lax.all_gather(field_in, 'row', axis=0, tiled=True))  36 us
  transfers between devices with their start and end apart: 10, of which 9 were waited for; matrix products, arithmetic and copies ran while one was open for 7% of the time, Pallas kernels for 0%

commit v1 on v0

--- a/solution.py
+++ b/solution.py
@@ -5,6 +5,24 @@
 
 N = 12288
 sharpness = 12.0
+
+
+def ring_gather(array, axis, dim):
+    ways, here, step = (lax.axis_size(axis), lax.axis_index(axis), array.shape[dim])
+    shape = [n * ways if d == dim else n for d, n in enumerate(array.shape)]
+    full = lax.dynamic_update_slice_in_dim(
+        jnp.zeros(shape, array.dtype), array, here * step, axis=dim
+    )
+    going_up = going_down = array
+    for far in range(1, ways // 2 + 1):
+        going_up = lax.ppermute(going_up, axis, [(d, (d + 1) % ways) for d in range(ways)])
+        full = lax.dynamic_update_slice_in_dim(full, going_up, (here - far) % ways * step, axis=dim)
+        if 2 * far < ways:
+            going_down = lax.ppermute(going_down, axis, [(d, (d - 1) % ways) for d in range(ways)])
+            full = lax.dynamic_update_slice_in_dim(
+                full, going_down, (here + far) % ways * step, axis=dim
+            )
+    return full
 
 
 def standardize(series):
@@ -84,7 +102,7 @@
     def normal_apply(field_in):
         product = forward_add(lax.all_gather(field_in, "row", axis=0, tiled=True))
         product = lax.psum_scatter(product, "col", scatter_dimension=0, tiled=True)
-        returned = backward_add(lax.all_gather(product, "col", axis=0, tiled=True))
+        returned = backward_add(ring_gather(product, "col", 0))
         return lax.psum_scatter(returned, "row", scatter_dimension=0, tiled=True) / spectral_scale
 
     first_term = normal_apply(vectors) - vectors

time: 568 us -> 560 us (0.986)
  waiting for transfers between devices: 291 us -> 281 us
    all_gather x2 -> x0, waiting for transfers between devices: 42.1 us -> none  [normal_apply(): returned = backward_add(lax.all_gather(product, 'col', axis=0, tiled=True))]
    ppermute x0 -> x6, waiting for transfers between devices: none -> 32.4 us  [the longest x4 32.4 us: ring_gather(): lax.ppermute(going_up, axis, [(d, (d + 1) % ways) for d in range(ways)])]
    all_gather x1, waiting for transfers between devices: 57.5 us -> 65 us  [local(): shard_piece = lax.all_gather(z_own, 'row', axis=0, tiled=True)]
    all_gather x1, waiting for transfers between devices: 28.7 us -> 22.5 us  [local(): lax.all_gather(z_own, 'col', axis=0, tiled=True)]
  transfers between devices with their start and end apart: 10 -> 14, of which waited for: 9 -> 11; matrix products, arithmetic and copies ran while one was open for 7% -> 8% of each run, Pallas kernels for 0% -> 0%
where the time goes in v1:
time: 560 us; the launch traced here: 553 us
  waiting for transfers between devices  281 us (50%)
  matrix products  239 us (43%)
  between operations  14.6 us (3%)
  other arithmetic  8.3 us (1%)
  blocking collectives  6.21 us (1%)
    dot_general x2, matrix products, backward_add(): lax.dot_general(affinity, shard_piece, (((0,), (0,)), ((), ())), precisio...  128 us
    dot_general x2, matrix products, forward_add(): jnp.dot(affinity, shard_piece, precision=lax.Precision.HIGHEST, preferred...  69.6 us
    reduce_scatter x2, waiting for transfers between devices, normal_apply(): lax.psum_scatter(returned, 'row', scatter_dimension=0, tiled=True)  69.5 us
    all_gather x1, waiting for transfers between devices, local(): shard_piece = lax.all_gather(z_own, 'row', axis=0, tiled=True)  65 us
    reduce_scatter x2, waiting for transfers between devices, normal_apply(): product = lax.psum_scatter(product, 'col', scatter_dimension=0, tiled=True)  53.7 us
    dot_general x1, matrix products, local(): lax.dot_general(z_rows, shard_piece, (((1,), (1,)), ((), ())), precision=...  40.2 us
    all_gather x2, waiting for transfers between devices, normal_apply(): product = forward_add(lax.all_gather(field_in, 'row', axis=0, tiled=True))  36 us
    ppermute x4, waiting for transfers between devices, ring_gather(): lax.ppermute(going_up, axis, [(d, (d + 1) % ways) for d in range(ways)])  32.4 us
  transfers between devices with their start and end apart: 14, of which 11 were waited for; matrix products, arithmetic and copies ran while one was open for 8% of the time, Pallas kernels for 0%

profile of v1, /device:TPU:0, one launch (start us, length us, event | category | flops | bytes accessed | tf_op | source)
XLA Modules:
  0.0 552.7 jit_solution(3224318714162124331)
XLA Ops:
  6.5 1.4 reduce_sum.36
  7.9 1.4 multiply_reduce_fusion
  9.4 1.2 subtract_multiply_fusion
  10.7 0.7 all-gather.8.cloned.1.call-update
  11.4 0.7 all-gather.10.cloned.1.call-update
  12.2 0.1 select_reduce_fusion
  12.3 6.2 %all-gather = f32[4,1,768]{2,1,0:T(1,128)S(1)} all-gather(f32[1,1,768]{2,1,0:T(1,128)S(1)} %reshape.49), channel_id=1, replica_groups=mesh['ens'=2,'row'=4,'col'=4] {'col'}, dimensions={0}, use_global_device_ids=true | all-gather | bytes 15360 | tf_op jit(solution)/shard_map/all_gather | solution.py:48
  18.5 0.9 fusion.1
  19.4 22.5 %all-gather.6.cloned.1.call-done = f32[3072,256]{1,0:T(8,128)} async-done(((f32[768,256]{1,0:T(8,128)}), f32[3072,256]{1,0:T(8,128)}) %all-gather.6.cloned.1.call-update) | async-done | bytes 3145744 | tf_op jit(solution)/shard_map/all_gather | solution.py:47
  42.0 65.0 %all-gather.8.cloned.1.call-done = f32[3072,256]{1,0:T(8,128)} async-done(((f32[768,256]{1,0:T(8,128)}), f32[3072,256]{1,0:T(8,128)}) %all-gather.8.cloned.1.call-update) | async-done | bytes 3145744 | tf_op jit(solution)/shard_map/all_gather | solution.py:57
  107.0 40.2 %fusion = f32[3072,3072]{1,0:T(8,128)} fusion(f32[3072,256]{1,0:T(8,128)} %all-gather.6.cloned.1.call-done, f32[3072,256]{1,0:T(8,128)} %all-gather.8.cloned.1.call-done, f32[3072]{0:T(1024)S(1)} %bitcast.15, f32[8,3072]{1,0:T(8,128)S(1)} %fusion.1), kind=kOutput, calls=%fused_computation.1 | convolution fusion | flops 29019340800 | bytes 44150784 | tf_op jit(solution)/shard_map/dot_general | solution.py:73
  147.2 34.9 %fusion.21 = f32[3072,128]{1,0:T(8,128)} fusion(f32[3072,3072]{1,0:T(8,128)} %fusion, f32[3072,128]{1,0:T(8,128)} %all-gather.10.cloned.1.call-done), kind=kOutput, calls=%fused_computation.47 | convolution fusion | flops 14495514624 | bytes 40894464 | tf_op jit(solution)/shard_map/dot_general | solution.py:86
  182.2 26.8 %reduce-scatter.5.cloned.1.call-done = f32[768,128]{1,0:T(8,128)} async-done(((f32[3072,128]{1,0:T(8,128)}), f32[768,128]{1,0:T(8,128)}) %reduce-scatter.5.cloned.1.call-update) | async-done | bytes 393232 | tf_op jit(solution)/shard_map/reduce_scatter | solution.py:104
  208.9 1.7 collective-permute-start.1
  210.7 9.2 %collective-permute-done = f32[768,128]{1,0:T(8,128)S(1)} collective-permute-done((f32[768,128]{1,0:T(8,128)}, f32[768,128]{1,0:T(8,128)S(1)}, u32[]{:S(2)}, u32[]{:S(2)}) %collective-permute-start) | collective-permute-done | bytes 393248 | tf_op jit(solution)/shard_map/ppermute | solution.py:18
  219.9 0.1 broadcast.106.clone
  220.2 6.9 %collective-permute-done.2 = f32[768,128]{1,0:T(8,128)S(1)} collective-permute-done((f32[768,128]{1,0:T(8,128)S(1)}, f32[768,128]{1,0:T(8,128)S(1)}, u32[]{:S(2)}, u32[]{:S(2)}) %collective-permute-start.2) | collective-permute-done | bytes 393248 | tf_op jit(solution)/shard_map/ppermute | solution.py:18
  227.2 64.3 %fusion.22 = f32[3072,128]{1,0:T(8,128)} fusion(f32[3072,3072]{1,0:T(8,128)} %fusion, f32[3072,128]{1,0:T(8,128)S(1)} %constant_dynamic-update-slice_fusion.4), kind=kOutput, calls=%fused_computation.48 | convolution fusion | flops 14495514624 | bytes 40894464 | tf_op jit(solution)/shard_map/dot_general | solution.py:94
  291.5 0.0 all-gather.12.cloned.1.call-start
  291.5 0.6 multiply_reduce_fusion.1
  292.8 34.1 %reduce-scatter.7.cloned.1.call-done = f32[768,128]{1,0:T(8,128)} async-done(((f32[3072,128]{1,0:T(8,128)}), f32[768,128]{1,0:T(8,128)}) %reduce-scatter.7.cloned.1.call-update) | async-done | bytes 393232 | tf_op jit(solution)/shard_map/reduce_scatter | solution.py:106
  326.8 1.8 divide_subtract_fusion
  328.7 36.0 %all-gather.12.cloned.1.call-done = f32[3072,128]{1,0:T(8,128)} async-done(((f32[768,128]{1,0:T(8,128)}), f32[3072,128]{1,0:T(8,128)}) %all-gather.12.cloned.1.call-update) | async-done | bytes 1572880 | tf_op jit(solution)/shard_map/all_gather | solution.py:103
  364.7 34.7 %fusion.23 = f32[3072,128]{1,0:T(8,128)} fusion(f32[3072,3072]{1,0:T(8,128)} %fusion, f32[3072,128]{1,0:T(8,128)} %all-gather.12.cloned.1.call-done), kind=kOutput, calls=%fused_computation.49 | convolution fusion | flops 14495514624 | bytes 40894464 | tf_op jit(solution)/shard_map/dot_general | solution.py:86
  399.4 27.0 %reduce-scatter.9.cloned.1.call-done = f32[768,128]{1,0:T(8,128)} async-done(((f32[3072,128]{1,0:T(8,128)}), f32[768,128]{1,0:T(8,128)}) %reduce-scatter.9.cloned.1.call-update) | async-done | bytes 393232 | tf_op jit(solution)/shard_map/reduce_scatter | solution.py:104
  426.4 1.7 collective-permute-start.4
  428.2 9.2 %collective-permute-done.3 = f32[768,128]{1,0:T(8,128)S(1)} collective-permute-done((f32[768,128]{1,0:T(8,128)}, f32[768,128]{1,0:T(8,128)S(1)}, u32[]{:S(2)}, u32[]{:S(2)}) %collective-permute-start.3) | collective-permute-done | bytes 393248 | tf_op jit(solution)/shard_map/ppermute | solution.py:18
  437.4 0.1 broadcast.106
  437.6 6.9 %collective-permute-done.5 = f32[768,128]{1,0:T(8,128)S(1)} collective-permute-done((f32[768,128]{1,0:T(8,128)S(1)}, f32[768,128]{1,0:T(8,128)S(1)}, u32[]{:S(2)}, u32[]{:S(2)}) %collective-permute-start.5) | collective-permute-done | bytes 393248 | tf_op jit(solution)/shard_map/ppermute | solution.py:18
  444.6 63.8 %fusion.24 = f32[3072,128]{1,0:T(8,128)} fusion(f32[3072,3072]{1,0:T(8,128)} %fusion, f32[3072,128]{1,0:T(8,128)S(1)} %constant_dynamic-update-slice_fusion), kind=kOutput, calls=%fused_computation.50 | convolution fusion | flops 14495514624 | bytes 40894464 | tf_op jit(solution)/shard_map/dot_general | solution.py:94
  508.4 35.4 %reduce-scatter.11.cloned.1.call-done = f32[768,128]{1,0:T(8,128)} async-done(((f32[3072,128]{1,0:T(8,128)}), f32[768,128]{1,0:T(8,128)}) %reduce-scatter.11.cloned.1.call-update) | async-done | bytes 393232 | tf_op jit(solution)/shard_map/reduce_scatter | solution.py:106
  543.8 1.8 multiply_subtract_fusion
  (46 shorter events, 0.7 us)
Async XLA Ops:
  6.5 2.8 copy-start
  6.5 35.5 %all-gather.6.cloned.1.call-start = ((), (), s32[]{:S(2)}) async-start(), calls=%async_computation.4 | async-start | bytes 3932160 | tf_op jit(solution)/shard_map/all_gather | solution.py:47
  9.4 2.8 copy-start.5
  9.4 2.8 copy-start.6
  10.6 96.4 %all-gather.8.cloned.1.call-start = ((), (), s32[]{:S(2)}) async-start(), calls=%async_computation.5 | async-start | bytes 3932160 | tf_op jit(solution)/shard_map/all_gather | solution.py:57
  11.4 135.9 %all-gather.10.cloned.1.call-start = ((), (), s32[]{:S(2)}) async-start(), calls=%async_computation.6 | async-start | bytes 1966080 | tf_op jit(solution)/shard_map/all_gather | solution.py:103
  12.1 196.8 %reduce-scatter.5.cloned.1.call-start = ((), (), s32[]{:S(2)}) async-start(), calls=%async_computation.7 | async-start | bytes 1966080 | tf_op jit(solution)/shard_map/reduce_scatter | solution.py:104
  182.1 144.7 %reduce-scatter.7.cloned.1.call-start = ((), (), s32[]{:S(2)}) async-start(), calls=%async_computation.8 | async-start | bytes 1966080 | tf_op jit(solution)/shard_map/reduce_scatter | solution.py:106
  208.9 11.1 %copy-start.3 = (f32[768,128]{1,0:T(8,128)S(1)}, f32[768,128]{1,0:T(8,128)}, u32[]{:S(2)}) copy-start(f32[768,128]{1,0:T(8,128)} %reduce-scatter.5.cloned.1.call-done) | copy-start | bytes 1179652
  208.9 11.0 %collective-permute-start = (f32[768,128]{1,0:T(8,128)}, f32[768,128]{1,0:T(8,128)S(1)}, u32[]{:S(2)}, u32[]{:S(2)}) collective-permute-start(f32[768,128]{1,0:T(8,128)} %reduce-scatter.5.cloned.1.call-done), channel_id=1, source_target_pairs={{0,1},{1,2},{2,3},{3,0},{4,5},{5,6},{6,7},{7,4},{8,9},{9,10},{10,1... | collective-permute-start | bytes 1179656 | tf_op jit(solution)/shard_map/ppermute | solution.py:18
  208.9 11.2 %collective-permute-start.1 = (f32[768,128]{1,0:T(8,128)}, f32[768,128]{1,0:T(8,128)S(1)}, u32[]{:S(2)}, u32[]{:S(2)}) collective-permute-start(f32[768,128]{1,0:T(8,128)} %reduce-scatter.5.cloned.1.call-done), channel_id=1, source_target_pairs={{0,3},{1,0},{2,1},{3,2},{4,7},{5,4},{6,5},{7,6},{8,11},{9,8},{10,9... | collective-permute-start | bytes 1179656 | tf_op jit(solution)/shard_map/ppermute | solution.py:21
  219.9 7.2 %collective-permute-start.2 = (f32[768,128]{1,0:T(8,128)S(1)}, f32[768,128]{1,0:T(8,128)S(1)}, u32[]{:S(2)}, u32[]{:S(2)}) collective-permute-start(f32[768,128]{1,0:T(8,128)S(1)} %collective-permute-done), channel_id=1, source_target_pairs={{0,1},{1,2},{2,3},{3,0},{4,5},{5,6},{6,7},{7,4},{8,9},{9,10},{10,1... | collective-permute-start | bytes 1179656 | tf_op jit(solution)/shard_map/ppermute | solution.py:18
  291.4 35.4 %copy-start.1 = (f32[768,128]{1,0:T(8,128)S(1)}, f32[768,128]{1,0:T(8,128)}, u32[]{:S(2)}) copy-start(f32[768,128]{1,0:T(8,128)} %param.6) | copy-start | bytes 1179652
  291.5 73.2 %all-gather.12.cloned.1.call-start = ((), (), s32[]{:S(2)}) async-start(), calls=%async_computation.9 | async-start | bytes 1966080 | tf_op jit(solution)/shard_map/all_gather | solution.py:103
  328.7 97.8 %reduce-scatter.9.cloned.1.call-start = ((), (), s32[]{:S(2)}) async-start(), calls=%async_computation.10 | async-start | bytes 1966080 | tf_op jit(solution)/shard_map/reduce_scatter | solution.py:104
  399.4 144.4 %reduce-scatter.11.cloned.1.call-start = ((), (), s32[]{:S(2)}) async-start(), calls=%async_computation.11 | async-start | bytes 1966080 | tf_op jit(solution)/shard_map/reduce_scatter | solution.py:106
  426.4 11.1 %copy-start.4 = (f32[768,128]{1,0:T(8,128)S(1)}, f32[768,128]{1,0:T(8,128)}, u32[]{:S(2)}) copy-start(f32[768,128]{1,0:T(8,128)} %reduce-scatter.9.cloned.1.call-done) | copy-start | bytes 1179652
  426.4 11.0 %collective-permute-start.3 = (f32[768,128]{1,0:T(8,128)}, f32[768,128]{1,0:T(8,128)S(1)}, u32[]{:S(2)}, u32[]{:S(2)}) collective-permute-start(f32[768,128]{1,0:T(8,128)} %reduce-scatter.9.cloned.1.call-done), channel_id=1, source_target_pairs={{0,1},{1,2},{2,3},{3,0},{4,5},{5,6},{6,7},{7,4},{8,9},{9,10},{10,1... | collective-permute-start | bytes 1179656 | tf_op jit(solution)/shard_map/ppermute | solution.py:18
  426.4 11.2 %collective-permute-start.4 = (f32[768,128]{1,0:T(8,128)}, f32[768,128]{1,0:T(8,128)S(1)}, u32[]{:S(2)}, u32[]{:S(2)}) collective-permute-start(f32[768,128]{1,0:T(8,128)} %reduce-scatter.9.cloned.1.call-done), channel_id=1, source_target_pairs={{0,3},{1,0},{2,1},{3,2},{4,7},{5,4},{6,5},{7,6},{8,11},{9,8},{10,9... | collective-permute-start | bytes 1179656 | tf_op jit(solution)/shard_map/ppermute | solution.py:21
  437.4 7.2 %collective-permute-start.5 = (f32[768,128]{1,0:T(8,128)S(1)}, f32[768,128]{1,0:T(8,128)S(1)}, u32[]{:S(2)}, u32[]{:S(2)}) collective-permute-start(f32[768,128]{1,0:T(8,128)S(1)} %collective-permute-done.3), channel_id=1, source_target_pairs={{0,1},{1,2},{2,3},{3,0},{4,5},{5,6},{6,7},{7,4},{8,9},{9,10},{10,1... | collective-permute-start | bytes 1179656 | tf_op jit(solution)/shard_map/ppermute | solution.py:18
  508.4 35.4 %copy-start.2 = (f32[768,128]{1,0:T(8,128)S(1)}, f32[768,128]{1,0:T(8,128)}, u32[]{:S(2)}) copy-start(f32[768,128]{1,0:T(8,128)} %reduce-scatter.7.cloned.1.call-done) | copy-start | bytes 1179652
Sparse Core Ops, SparseCore 0:
  10.7 31.2 all-gather.5
  43.6 63.4 all-gather.7
  108.6 35.6 all-gather.9
  182.2 26.6 reduce-scatter.4
  291.6 35.1 reduce-scatter.6
  328.8 35.8 all-gather.11
  399.5 26.8 reduce-scatter.8
  508.5 35.2 reduce-scatter.10
